TPU v7x, 32 devices: a whole 2x2x4 slice. The times are simulated.
32 devices in a mesh: blk: 8 (over z, x), rep: 4 (over y, core).
Axes of the slice: x: 2, y: 2, z: 4, core: 2. Of those that a mesh axis runs over, the one named last changes fastest.
Arguments:
- points: bfloat16 [6144, 1024], P('blk'), may hold values from -6 to 6
- w_in: bfloat16 [1024, 512], replicated, may hold values from -0.1875 to 0.1875
- b_in: float32 [512], replicated, may hold values from -3 to 3
- w_out: bfloat16 [512, 64], replicated, may hold values from -0.25 to 0.25
- inv_scale: float32 [64], replicated, may hold values from 0.05 to 0.5
- solves: bfloat16 [64, 6144], P(None, 'blk'), may hold values from -1.6875 to 1.6875
- probes: bfloat16 [64, 6144], P(None, 'blk'), may hold values from -1.6875 to 1.6875
Outputs:
- feat_grad: float32 [64, 6144], P(None, ('blk', 'rep'))
- grad_w_in: float32 [1024, 512], replicated
- grad_b_in: float32 [512], replicated
- grad_w_out: float32 [512, 64], replicated
All inputs are finite; a program needn't handle non-finite values.
Results may differ from a plain program's by a relative error of at most 0.034.
Values may be sent and summed in bfloat16 or wider, within the bound.
No kernel may reach another device: no remote copies, remote signals or barrier semaphores. Data moves between devices by JAX's collectives and lax.ppermute only.
A program may use at most 64 MiB of HBM per device.

v0:
```python
import math
import jax
import jax.numpy as jnp
from jax import lax
from jax.sharding import PartitionSpec as P


def shifted(block, axis, distance):
    devices = range(lax.axis_size(axis))
    route = [((i - distance) % len(devices), i) for i in devices]
    return lax.ppermute(block, axis, route)


def couple(own_y, own_pair, own_sq, visitor, feat):
    vis_y = visitor[:feat]
    vis_pair = visitor[feat:]
    vis_sq = jnp.sum(jnp.square(vis_y.astype(jnp.float32)), axis=0)
    cross = lax.dot_general(
        own_y, vis_y, (((0,), (0,)), ((), ())), preferred_element_type=jnp.float32
    )
    kernel = jnp.exp(-0.5 * (own_sq[:, None] + vis_sq[None, :] - 2.0 * cross))
    coupling = lax.dot_general(
        own_pair, vis_pair, (((0,), (0,)), ((), ())), preferred_element_type=jnp.float32
    )
    weight_b = (coupling * kernel).astype(jnp.bfloat16)
    totals = jnp.sum(weight_b.astype(jnp.float32), axis=1)
    pull = lax.dot_general(
        vis_y, weight_b, (((1,), (1,)), ((), ())), preferred_element_type=jnp.float32
    )
    return (totals, pull)


def on_device(points, w_in, b_in, w_out, inv_scale, solves, probes):
    feat = w_out.shape[1]
    reps = lax.axis_size("rep")
    blocks = lax.axis_size("blk")
    rep_index = lax.axis_index("rep")
    rows = points.shape[0]
    quarter = rows // reps
    first = rep_index * quarter
    npts = rows * blocks
    levels = reps.bit_length() - 1
    own_points = lax.dynamic_slice_in_dim(points, first, quarter, 0)
    hidden = jnp.tanh(jnp.dot(points, w_in, preferred_element_type=jnp.float32) + b_in).astype(
        jnp.bfloat16
    )
    pre = lax.dot_general(
        w_out, hidden, (((0,), (1,)), ((), ())), preferred_element_type=jnp.float32
    )
    hidden, scaled = (hidden, (pre * inv_scale[:, None]).astype(jnp.bfloat16))
    own_hidden = lax.dynamic_slice_in_dim(hidden, first, quarter, 0)
    own_pair = jnp.concatenate([solves, probes], axis=0)
    own_sq = jnp.sum(jnp.square(scaled.astype(jnp.float32)), axis=0)
    scaled32 = scaled.astype(jnp.float32)
    visitor = jnp.concatenate([scaled, probes, solves], axis=0)
    for bit in range(levels):
        moved = shifted(visitor, "blk", -(1 << bit))
        visitor = jnp.where(rep_index // (1 << bit) % 2 == 1, moved, visitor)

    def accumulate(state, vis):
        totals, pull = couple(scaled, own_pair, own_sq, vis, feat)
        return (state[0] + totals, state[1] + pull)

    init = (jnp.zeros((rows,), jnp.float32), jnp.zeros((feat, rows), jnp.float32))
    steps = blocks // reps

    def advance(index, carry):
        state, vis = carry
        state = accumulate(state, vis)
        return (state, shifted(vis, "blk", -reps))

    state, last_vis = lax.fori_loop(0, steps - 1, advance, (init, visitor))
    state = accumulate(state, last_vis)
    totals, pull = state
    drift = pull - scaled32 * totals[None, :]
    summed = lax.psum_scatter(drift, "rep", scatter_dimension=1, tiled=True)
    feat_grad = summed * inv_scale[:, None]
    grad_b16 = feat_grad.astype(jnp.bfloat16)
    back = lax.dot_general(
        grad_b16, w_out, (((0,), (1,)), ((), ())), preferred_element_type=jnp.float32
    )
    hid32 = own_hidden.astype(jnp.float32)
    pre_grad = back * (1.0 - hid32 * hid32)
    norm = 1.0 / math.sqrt(npts)
    term_w_in = (
        lax.dot_general(
            own_points,
            pre_grad.astype(jnp.bfloat16),
            (((0,), (0,)), ((), ())),
            preferred_element_type=jnp.float32,
        )
        * norm
    )
    term_b_in = jnp.sum(pre_grad, axis=0) * norm
    term_w_out = (
        lax.dot_general(
            own_hidden, grad_b16, (((0,), (1,)), ((), ())), preferred_element_type=jnp.float32
        )
        * norm
    )
    grad_w_in, grad_b_in, grad_w_out = lax.psum((term_w_in, term_b_in, term_w_out), ("blk", "rep"))
    return (feat_grad, grad_w_in, grad_b_in, grad_w_out)


def solution(mesh):
    in_specs = (P("blk", None), P(), P(), P(), P(), P(None, "blk"), P(None, "blk"))
    out_specs = (P(None, ("blk", "rep")), P(), P(), P())
    return jax.shard_map(
        on_device, mesh=mesh, in_specs=in_specs, out_specs=out_specs, check_vma=False
    )
```

profile of v0, /device:TPU:0, one launch (start us, length us, event | category | flops | bytes accessed | tf_op | source)
XLA Modules:
  0.0 224.5 jit_solution(10279714449616067677)
XLA Ops:
  7.2 0.0 copy-start
  7.2 0.0 copy-start.6
  7.2 0.0 copy-start.5
  7.2 0.0 copy-start.1
  7.2 0.0 copy-start.2
  7.2 0.0 reduce-scatter.4.cloned.1.call-start
  7.3 1.3 copy-done
  8.6 2.2 tanh_convert_fusion
  10.8 0.0 copy-done.6
  10.8 0.0 copy-done.5
  10.8 0.4 fusion.3
  11.2 0.0 copy-done.1
  11.2 0.0 copy-done.2
  11.2 6.1 %collective-permute-start = (bf16[192,768]{1,0:T(8,128)(2,1)S(1)}, bf16[192,768]{1,0:T(8,128)(2,1)S(1)}, u32[]{:S(2)}, u32[]{:S(2)}) collective-permute-start(bf16[192,768]{1,0:T(8,128)(2,1)S(1)} %pad_maximum_fusion), channel_id=1, source_target_pairs={{4,0},{8,4},{12,8},{16,12},{20,16},{24,20},{28,24},{0,28},{5,1},{9... | collective-permute-start | bytes 884744 | tf_op jit(solution)/shard_map/ppermute | solution.py:11
  17.3 6.3 %collective-permute-done = bf16[192,768]{1,0:T(8,128)(2,1)S(1)} collective-permute-done((bf16[192,768]{1,0:T(8,128)(2,1)S(1)}, bf16[192,768]{1,0:T(8,128)(2,1)S(1)}, u32[]{:S(2)}, u32[]{:S(2)}) %collective-permute-start) | collective-permute-done | bytes 294944 | tf_op jit(solution)/shard_map/ppermute | solution.py:11
  23.6 0.1 broadcast_select_fusion
  23.6 1.6 collective-permute-start.1
  25.3 6.3 %collective-permute-done.1 = bf16[192,768]{1,0:T(8,128)(2,1)S(1)} collective-permute-done((bf16[192,768]{1,0:T(8,128)(2,1)S(1)}, bf16[192,768]{1,0:T(8,128)(2,1)S(1)}, u32[]{:S(2)}, u32[]{:S(2)}) %collective-permute-start.1) | collective-permute-done | bytes 294944 | tf_op jit(solution)/shard_map/ppermute | solution.py:11
  31.6 0.6 collective-permute-start.2
  32.3 0.5 fusion.13
  32.8 0.9 convert_reduce_fusion.1
  33.7 12.2 %collective-permute-done.2 = bf16[192,768]{1,0:T(8,128)(2,1)S(1)} collective-permute-done((bf16[192,768]{1,0:T(8,128)(2,1)S(1)}, bf16[192,768]{1,0:T(8,128)(2,1)S(1)}, u32[]{:S(2)}, u32[]{:S(2)}) %collective-permute-start.2) | collective-permute-done | bytes 294944 | tf_op jit(solution)/shard_map/while/body/eval_jaxpr/ppermute | solution.py:11
  46.0 0.5 fusion.10
  46.5 0.9 convert_reduce_fusion
  47.4 0.3 fusion.8
  47.8 0.3 fusion
  48.1 0.9 copy.11
  49.0 0.0 reduce-scatter.4.cloned.1.call-update
  49.1 0.0 all-reduce.3.cloned.1.call-start
  49.1 22.9 %reduce-scatter.4.cloned.1.call-done = f32[192,64]{1,0:T(8,128)} async-done(((f32[768,64]{1,0:T(8,128)}), f32[192,64]{1,0:T(8,128)}) %reduce-scatter.4.cloned.1.call-update) | async-done | bytes 49168
  72.0 1.0 copy.12
  73.0 0.1 broadcast_multiply_fusion
  73.0 0.0 copy-start.3
  73.0 0.3 fusion.19
  73.3 0.8 convolution_multiply_fusion.3
  74.1 1.8 convolution_multiply_fusion
  75.9 0.0 all-reduce.3.cloned.1.call-update
  75.9 0.0 copy-done.3
  76.0 39.6 %psum.22 = f32[512]{0:T(512)} all-reduce(f32[512]{0:T(512)S(1)} %broadcast_multiply_fusion.1), channel_id=1, replica_groups=mesh['blk'=8,'rep'=4] {'blk','rep'}, use_global_device_ids=true, to_apply=%region_8.9 | all-reduce | flops 512 | bytes 4096 | tf_op jit(solution)/shard_map/psum | solution.py:101
  115.6 98.3 %all-reduce.3.cloned.1.call-done = (f32[1024,512]{1,0:T(8,128)}, f32[512,64]{0,1:T(8,128)}) async-done(((f32[1024,512]{1,0:T(8,128)}, f32[512,64]{0,1:T(8,128)}), (f32[1024,512]{1,0:T(8,128)}, f32[512,64]{0,1:T(8,128)})) %all-reduce.3.cloned.1.call-update) | async-done | bytes 2228240 | tf_op jit(solution)/shard_map/psum | solution.py:101
  213.9 0.0 copy-start.4
  213.9 3.1 %copy.16 = f32[1024,512]{1,0:T(8,128)} copy(f32[1024,512]{1,0:T(8,128)} %get-tuple-element.38) | data formatting | bytes 4194304
  217.0 0.0 copy-done.4
  217.0 0.7 copy.17
  (8 shorter events, 0.1 us)
Async XLA Ops:
  7.2 1.4 copy-start
  7.2 3.6 %copy-start.6 = (f32[64]{0:T(128)S(1)}, f32[64]{0:T(128)}, u32[]{:S(2)}) copy-start(f32[64]{0:T(128)} %param.11) | copy-start | bytes 772
  7.2 3.6 %copy-start.5 = (bf16[512,64]{0,1:T(8,128)(2,1)S(1)}, bf16[512,64]{0,1:T(8,128)(2,1)}, u32[]{:S(2)}) copy-start(bf16[512,64]{0,1:T(8,128)(2,1)} %param.10) | copy-start | bytes 196612
  7.2 4.0 %copy-start.1 = (bf16[64,768]{1,0:T(8,128)(2,1)S(1)}, bf16[64,768]{1,0:T(8,128)(2,1)}, u32[]{:S(2)}) copy-start(bf16[64,768]{1,0:T(8,128)(2,1)} %param.12) | copy-start | bytes 294916
  7.2 4.0 %copy-start.2 = (bf16[64,768]{1,0:T(8,128)(2,1)S(1)}, bf16[64,768]{1,0:T(8,128)(2,1)}, u32[]{:S(2)}) copy-start(bf16[64,768]{1,0:T(8,128)(2,1)} %param.13) | copy-start | bytes 294916
  7.2 64.8 %reduce-scatter.4.cloned.1.call-start = ((), (), s32[]{:S(2)}) async-start(), calls=%async_computation.1 | async-start | bytes 491520
  11.2 12.3 %collective-permute-start = (bf16[192,768]{1,0:T(8,128)(2,1)S(1)}, bf16[192,768]{1,0:T(8,128)(2,1)S(1)}, u32[]{:S(2)}, u32[]{:S(2)}) collective-permute-start(bf16[192,768]{1,0:T(8,128)(2,1)S(1)} %pad_maximum_fusion), channel_id=1, source_target_pairs={{4,0},{8,4},{12,8},{16,12},{20,16},{24,20},{28,24},{0,28},{5,1},{9... | collective-permute-start | bytes 884744 | tf_op jit(solution)/shard_map/ppermute | solution.py:11
  23.6 7.9 %collective-permute-start.1 = (bf16[192,768]{1,0:T(8,128)(2,1)S(1)}, bf16[192,768]{1,0:T(8,128)(2,1)S(1)}, u32[]{:S(2)}, u32[]{:S(2)}) collective-permute-start(bf16[192,768]{1,0:T(8,128)(2,1)S(1)} %broadcast_select_fusion), channel_id=1, source_target_pairs={{8,0},{12,4},{16,8},{20,12},{24,16},{28,20},{0,24},{4,28},{9,1},{1... | collective-permute-start | bytes 884744 | tf_op jit(solution)/shard_map/ppermute | solution.py:11
  31.6 14.3 %collective-permute-start.2 = (bf16[192,768]{1,0:T(8,128)(2,1)S(1)}, bf16[192,768]{1,0:T(8,128)(2,1)S(1)}, u32[]{:S(2)}, u32[]{:S(2)}) collective-permute-start(bf16[192,768]{1,0:T(8,128)(2,1)S(1)} %broadcast_select_fusion.1), channel_id=1, source_target_pairs={{16,0},{20,4},{24,8},{28,12},{0,16},{4,20},{8,24},{12,28},{17,1},{... | collective-permute-start | bytes 884744 | tf_op jit(solution)/shard_map/while/body/eval_jaxpr/ppermute | solution.py:11
  49.1 164.8 %all-reduce.3.cloned.1.call-start = ((), (), s32[]{:S(2)}) async-start(), calls=%async_computation.2 | async-start | bytes 4456448 | tf_op jit(solution)/shard_map/psum | solution.py:101
  73.0 2.9 %copy-start.3 = (f32[64,192]{1,0:T(8,128)}, f32[64,192]{1,0:T(8,128)S(1)}, u32[]{:S(2)}) copy-start(f32[64,192]{1,0:T(8,128)S(1)} %broadcast_multiply_fusion) | copy-start | bytes 147460
  213.9 3.1 %copy-start.4 = (f32[512,64]{0,1:T(8,128)S(1)}, f32[512,64]{0,1:T(8,128)}, u32[]{:S(2)}) copy-start(f32[512,64]{0,1:T(8,128)} %get-tuple-element.40) | copy-start | bytes 393220
Sparse Core Ops, SparseCore 0:
  49.2 22.7 reduce-scatter.3
  78.1 135.7 all-reduce.2
where the time goes:
time: 225 us; the launch traced here: 224 us
  waiting for transfers between devices  146 us (65%)
  blocking collectives  39.6 us (18%)
  between operations  14.2 us (6%)
  matrix products  8.95 us (4%)
  starting transfers between devices  8.36 us (4%)
  local copies, waits for them, and re-layouts  7.02 us (3%)
    psum x1, waiting for transfers between devices, on_device(): lax.psum((term_w_in, term_b_in, term_w_out), ('blk', 'rep'))  98.3 us
    psum x1, blocking collectives, on_device(): lax.psum((term_w_in, term_b_in, term_w_out), ('blk', 'rep'))  39.6 us
    ppermute x3, waiting for transfers between devices, shifted(): return lax.ppermute(block, axis, route)  24.8 us
    unnamed x3, waiting for transfers between devices  22.9 us
    ppermute x3, starting transfers between devices, shifted(): return lax.ppermute(block, axis, route)  8.29 us
    unnamed x19, local copies, waits for them, and re-layouts  7.01 us
  transfers between devices with their start and end apart: 5, of which 5 were waited for; matrix products, arithmetic and copies ran while one was open for 1% of the time, Pallas kernels for 0%

commit v1 on v0

--- a/solution.py
+++ b/solution.py
@@ -98,7 +98,9 @@
         )
         * norm
     )
-    grad_w_in, grad_b_in, grad_w_out = lax.psum((term_w_in, term_b_in, term_w_out), ("blk", "rep"))
+    grad_w_in, grad_b_in, grad_w_out = lax.psum(
+        lax.psum((term_w_in, term_b_in, term_w_out), "rep"), "blk"
+    )
     return (feat_grad, grad_w_in, grad_b_in, grad_w_out)
 
 

time: 225 us -> 250 us (1.11)
  waiting for transfers between devices: 146 us -> 183 us
  blocking collectives: 39.6 us -> 28.6 us
    psum x1 -> x2, waiting for transfers between devices: 98.3 us -> 135 us  [the longest x1 81.2 us: on_device(): lax.psum(lax.psum((term_w_in, term_b_in, term_w_out), 'rep'), 'blk')]
    psum x1 -> x2, blocking collectives: 39.6 us -> 28.6 us  [the longest x1 22.8 us: on_device(): lax.psum(lax.psum((term_w_in, term_b_in, term_w_out), 'rep'), 'blk')]
    unnamed x3 -> x4, waiting for transfers between devices: 22.9 us -> 22.9 us
  transfers between devices with their start and end apart: 5 -> 6, of which waited for: 5 -> 6; matrix products, arithmetic and copies ran while one was open for 1% -> 1% of each run, Pallas kernels for 0% -> 0%
where the time goes in v1:
time: 250 us
  waiting for transfers between devices  183 us (73%)
  blocking collectives  28.6 us (11%)
  between operations  13.9 us (6%)
  matrix products  8.95 us (4%)
  starting transfers between devices  8.41 us (3%)
  local copies, waits for them, and re-layouts  7.02 us (3%)
    psum x1, waiting for transfers between devices, on_device(): lax.psum(lax.psum((term_w_in, term_b_in, term_w_out), 'rep'), 'blk')  81.2 us
    psum x1, waiting for transfers between devices, on_device(): lax.psum((term_w_in, term_b_in, term_w_out), 'rep')  53.6 us
    ppermute x3, waiting for transfers between devices, shifted(): return lax.ppermute(block, axis, route)  24.8 us
    unnamed x4, waiting for transfers between devices  22.9 us
    psum x1, blocking collectives, on_device(): lax.psum(lax.psum((term_w_in, term_b_in, term_w_out), 'rep'), 'blk')  22.8 us
    ppermute x3, starting transfers between devices, shifted(): return lax.ppermute(block, axis, route)  8.29 us
    unnamed x19, local copies, waits for them, and re-layouts  7.01 us
    psum x1, blocking collectives, on_device(): lax.psum((term_w_in, term_b_in, term_w_out), 'rep')  5.8 us
  transfers between devices with their start and end apart: 6, of which 6 were waited for; matrix products, arithmetic and copies ran while one was open for 1% of the time, Pallas kernels for 0%

profile of v1, /device:TPU:0, one launch (start us, length us, event | category | flops | bytes accessed | tf_op | source)
XLA Modules:
  0.0 249.8 jit_solution(6843363047166773124)
XLA Ops:
  7.2 0.0 copy-start
  7.2 0.0 copy-start.6
  7.2 0.0 copy-start.5
  7.2 0.0 copy-start.1
  7.2 0.0 copy-start.2
  7.2 0.0 reduce-scatter.4.cloned.1.call-start
  7.3 1.3 copy-done
  8.6 2.2 tanh_convert_fusion
  10.8 0.0 copy-done.6
  10.8 0.0 copy-done.5
  10.8 0.4 fusion.3
  11.2 0.0 copy-done.1
  11.2 0.0 copy-done.2
  11.2 6.1 %collective-permute-start = (bf16[192,768]{1,0:T(8,128)(2,1)S(1)}, bf16[192,768]{1,0:T(8,128)(2,1)S(1)}, u32[]{:S(2)}, u32[]{:S(2)}) collective-permute-start(bf16[192,768]{1,0:T(8,128)(2,1)S(1)} %pad_maximum_fusion), channel_id=1, source_target_pairs={{4,0},{8,4},{12,8},{16,12},{20,16},{24,20},{28,24},{0,28},{5,1},{9... | collective-permute-start | bytes 884744 | tf_op jit(solution)/shard_map/ppermute | solution.py:11
  17.3 6.3 %collective-permute-done = bf16[192,768]{1,0:T(8,128)(2,1)S(1)} collective-permute-done((bf16[192,768]{1,0:T(8,128)(2,1)S(1)}, bf16[192,768]{1,0:T(8,128)(2,1)S(1)}, u32[]{:S(2)}, u32[]{:S(2)}) %collective-permute-start) | collective-permute-done | bytes 294944 | tf_op jit(solution)/shard_map/ppermute | solution.py:11
  23.6 0.1 broadcast_select_fusion
  23.6 1.6 collective-permute-start.1
  25.3 6.3 %collective-permute-done.1 = bf16[192,768]{1,0:T(8,128)(2,1)S(1)} collective-permute-done((bf16[192,768]{1,0:T(8,128)(2,1)S(1)}, bf16[192,768]{1,0:T(8,128)(2,1)S(1)}, u32[]{:S(2)}, u32[]{:S(2)}) %collective-permute-start.1) | collective-permute-done | bytes 294944 | tf_op jit(solution)/shard_map/ppermute | solution.py:11
  31.6 0.6 collective-permute-start.2
  32.3 0.5 fusion.13
  32.8 0.9 convert_reduce_fusion.1
  33.7 12.2 %collective-permute-done.2 = bf16[192,768]{1,0:T(8,128)(2,1)S(1)} collective-permute-done((bf16[192,768]{1,0:T(8,128)(2,1)S(1)}, bf16[192,768]{1,0:T(8,128)(2,1)S(1)}, u32[]{:S(2)}, u32[]{:S(2)}) %collective-permute-start.2) | collective-permute-done | bytes 294944 | tf_op jit(solution)/shard_map/while/body/eval_jaxpr/ppermute | solution.py:11
  46.0 0.5 fusion.10
  46.5 0.9 convert_reduce_fusion
  47.4 0.3 fusion.8
  47.8 0.3 fusion
  48.1 0.9 copy.11
  49.0 0.0 reduce-scatter.4.cloned.1.call-update
  49.1 0.0 all-reduce.7.cloned.1.call-start
  49.1 22.9 %reduce-scatter.4.cloned.1.call-done = f32[192,64]{1,0:T(8,128)} async-done(((f32[768,64]{1,0:T(8,128)}), f32[192,64]{1,0:T(8,128)}) %reduce-scatter.4.cloned.1.call-update) | async-done | bytes 49168
  72.0 1.0 copy.12
  73.0 0.1 broadcast_multiply_fusion
  73.0 0.0 copy-start.3
  73.0 0.3 fusion.19
  73.3 0.8 convolution_multiply_fusion.3
  74.1 1.8 convolution_multiply_fusion
  75.9 0.0 all-reduce.7.cloned.1.call-update
  75.9 0.0 copy-done.3
  75.9 0.0 all-reduce.5.cloned.1.call-start
  76.0 53.6 %all-reduce.7.cloned.1.call-done = (f32[1024,512]{1,0:T(8,128)}, f32[512,64]{0,1:T(8,128)}) async-done(((f32[1024,512]{1,0:T(8,128)}, f32[512,64]{0,1:T(8,128)}), (f32[1024,512]{1,0:T(8,128)}, f32[512,64]{0,1:T(8,128)})) %all-reduce.7.cloned.1.call-update) | async-done | bytes 2228240 | tf_op jit(solution)/shard_map/psum | solution.py:102
  129.6 0.0 all-reduce.5.cloned.1.call-update
  129.7 5.8 %psum.44 = f32[512]{0:T(512)S(1)} all-reduce(f32[512]{0:T(512)S(1)} %broadcast_multiply_fusion.1), channel_id=1, replica_groups=mesh['blk'=8,'rep'=4] {'rep'}, use_global_device_ids=true, to_apply=%region_9.10 | all-reduce | flops 512 | bytes 4096 | tf_op jit(solution)/shard_map/psum | solution.py:102
  135.5 22.8 %psum.45 = f32[512]{0:T(512)} all-reduce(f32[512]{0:T(512)S(1)} %psum.44), channel_id=1, replica_groups=mesh['blk'=8,'rep'=4] {'blk'}, use_global_device_ids=true, to_apply=%region_10.11 | all-reduce | flops 512 | bytes 4096 | tf_op jit(solution)/shard_map/psum | solution.py:101
  158.3 81.2 %all-reduce.5.cloned.1.call-done = (f32[1024,512]{1,0:T(8,128)}, f32[512,64]{0,1:T(8,128)}) async-done(((f32[1024,512]{1,0:T(8,128)}, f32[512,64]{0,1:T(8,128)}), (f32[1024,512]{1,0:T(8,128)}, f32[512,64]{0,1:T(8,128)})) %all-reduce.5.cloned.1.call-update) | async-done | bytes 2228240 | tf_op jit(solution)/shard_map/psum | solution.py:101
  239.5 0.0 copy-start.4
  239.5 3.1 %copy.18 = f32[1024,512]{1,0:T(8,128)} copy(f32[1024,512]{1,0:T(8,128)} %get-tuple-element.40) | data formatting | bytes 4194304
  242.6 0.0 copy-done.4
  242.6 0.7 copy.19
  (8 shorter events, 0.1 us)
Async XLA Ops:
  7.2 1.4 copy-start
  7.2 3.6 %copy-start.6 = (f32[64]{0:T(128)S(1)}, f32[64]{0:T(128)}, u32[]{:S(2)}) copy-start(f32[64]{0:T(128)} %param.11) | copy-start | bytes 772
  7.2 3.6 %copy-start.5 = (bf16[512,64]{0,1:T(8,128)(2,1)S(1)}, bf16[512,64]{0,1:T(8,128)(2,1)}, u32[]{:S(2)}) copy-start(bf16[512,64]{0,1:T(8,128)(2,1)} %param.10) | copy-start | bytes 196612
  7.2 4.0 %copy-start.1 = (bf16[64,768]{1,0:T(8,128)(2,1)S(1)}, bf16[64,768]{1,0:T(8,128)(2,1)}, u32[]{:S(2)}) copy-start(bf16[64,768]{1,0:T(8,128)(2,1)} %param.12) | copy-start | bytes 294916
  7.2 4.0 %copy-start.2 = (bf16[64,768]{1,0:T(8,128)(2,1)S(1)}, bf16[64,768]{1,0:T(8,128)(2,1)}, u32[]{:S(2)}) copy-start(bf16[64,768]{1,0:T(8,128)(2,1)} %param.13) | copy-start | bytes 294916
  7.2 64.8 %reduce-scatter.4.cloned.1.call-start = ((), (), s32[]{:S(2)}) async-start(), calls=%async_computation.1 | async-start | bytes 491520
  11.2 12.3 %collective-permute-start = (bf16[192,768]{1,0:T(8,128)(2,1)S(1)}, bf16[192,768]{1,0:T(8,128)(2,1)S(1)}, u32[]{:S(2)}, u32[]{:S(2)}) collective-permute-start(bf16[192,768]{1,0:T(8,128)(2,1)S(1)} %pad_maximum_fusion), channel_id=1, source_target_pairs={{4,0},{8,4},{12,8},{16,12},{20,16},{24,20},{28,24},{0,28},{5,1},{9... | collective-permute-start | bytes 884744 | tf_op jit(solution)/shard_map/ppermute | solution.py:11
  23.6 7.9 %collective-permute-start.1 = (bf16[192,768]{1,0:T(8,128)(2,1)S(1)}, bf16[192,768]{1,0:T(8,128)(2,1)S(1)}, u32[]{:S(2)}, u32[]{:S(2)}) collective-permute-start(bf16[192,768]{1,0:T(8,128)(2,1)S(1)} %broadcast_select_fusion), channel_id=1, source_target_pairs={{8,0},{12,4},{16,8},{20,12},{24,16},{28,20},{0,24},{4,28},{9,1},{1... | collective-permute-start | bytes 884744 | tf_op jit(solution)/shard_map/ppermute | solution.py:11
  31.6 14.3 %collective-permute-start.2 = (bf16[192,768]{1,0:T(8,128)(2,1)S(1)}, bf16[192,768]{1,0:T(8,128)(2,1)S(1)}, u32[]{:S(2)}, u32[]{:S(2)}) collective-permute-start(bf16[192,768]{1,0:T(8,128)(2,1)S(1)} %broadcast_select_fusion.1), channel_id=1, source_target_pairs={{16,0},{20,4},{24,8},{28,12},{0,16},{4,20},{8,24},{12,28},{17,1},{... | collective-permute-start | bytes 884744 | tf_op jit(solution)/shard_map/while/body/eval_jaxpr/ppermute | solution.py:11
  49.1 80.6 %all-reduce.7.cloned.1.call-start = ((), (), s32[]{:S(2)}) async-start(), calls=%async_computation.3 | async-start | bytes 4456448 | tf_op jit(solution)/shard_map/psum | solution.py:102
  73.0 2.9 %copy-start.3 = (f32[64,192]{1,0:T(8,128)}, f32[64,192]{1,0:T(8,128)S(1)}, u32[]{:S(2)}) copy-start(f32[64,192]{1,0:T(8,128)S(1)} %broadcast_multiply_fusion) | copy-start | bytes 147460
  75.9 163.6 %all-reduce.5.cloned.1.call-start = ((), (), s32[]{:S(2)}) async-start(), calls=%async_computation.2 | async-start | bytes 4456448 | tf_op jit(solution)/shard_map/psum | solution.py:101
  239.5 3.1 %copy-start.4 = (f32[512,64]{0,1:T(8,128)S(1)}, f32[512,64]{0,1:T(8,128)}, u32[]{:S(2)}) copy-start(f32[512,64]{0,1:T(8,128)} %get-tuple-element.42) | copy-start | bytes 393220
Sparse Core Ops, SparseCore 0:
  49.2 22.7 reduce-scatter.3
  76.1 53.5 all-reduce.6
  133.3 106.1 all-reduce.4
